TPU v7x, 32 devices: a whole 2x2x4 slice. The times are simulated.
32 devices in a mesh: tm: 16 (over z, y, x), col: 2 (over core).
Axes of the slice: x: 2, y: 2, z: 4, core: 2. Of those that a mesh axis runs over, the one named last changes fastest.
Arguments:
- diagonal_blocks: float32 [32, 512, 512], P('tm', 'col'), as said below
- upper_blocks: float32 [32, 512, 512], P('tm', 'col')
- right_sides: float32 [32, 512, 512], P('tm', 'col'), may hold values from -6 to 6
Outputs:
- reduced_blocks: float32 [32, 512, 512], P('tm', 'col')
- reduced_uppers: float32 [32, 512, 512], P('tm', 'col')
- reduced_sources: float32 [32, 512, 512], P('tm', 'col')
Inputs may be any that keep to these rules, and one draw needn't show every extreme that they name: `diagonal_blocks`: every block is symmetric, and the block-tridiagonal matrix built from these blocks and upper_blocks is positive definite.
All inputs are finite; a program needn't handle non-finite values.
Results may differ from a plain program's by a relative error of at most 0.0001.
Values sent between devices are 32-bit elements; how exact they have to be, the bound alone decides.
A program may use at most 64 MiB of HBM per device.

v0:
```python
import functools

import jax
import jax.numpy as jnp
from jax import lax
from jax.experimental import pallas as pl
from jax.experimental.pallas import tpu as pltpu
from jax.sharding import PartitionSpec as P

LEVELS = 2
TILE = 128
PANEL = 8
F32 = jnp.float32
BF16 = jnp.bfloat16


def split(values):
    high = values.astype(BF16)
    return high, (values - high.astype(F32)).astype(BF16)


def dot_parts(left, right, dims):
    def one(a, b):
        return lax.dot_general(a, b, (dims, ((), ())), preferred_element_type=F32)

    return one(left[0], right[0]) + (one(left[0], right[1]) + one(left[1], right[0]))


def dot3(left, right, dims=((1,), (0,))):
    return dot_parts(split(left), split(right), dims)


def dot6(left, right):
    return jnp.dot(left, right, precision=lax.Precision.HIGHEST, preferred_element_type=F32)


def panel_step(a):
    size = a.shape[0]
    lanes = lax.broadcasted_iota(jnp.int32, (PANEL, size), 1)
    subs = lax.broadcasted_iota(jnp.int32, (PANEL, size), 0)
    cols = [jnp.broadcast_to(a[:, i : i + 1], (size, size)) for i in range(PANEL)]
    rows = [
        jnp.where(
            lanes < PANEL,
            jnp.where(lanes == i, 1.0, 0.0),
            jnp.broadcast_to(a[i : i + 1, :], (PANEL, size)),
        )
        for i in range(PANEL)
    ]
    s = [
        [jnp.broadcast_to(cols[j][i : i + 1, :], (PANEL, size)) if j >= i else None for j in range(PANEL)]
        for i in range(PANEL)
    ]
    scale = [None] * PANEL
    low = {}
    for k in range(PANEL):
        scale[k] = 1.0 / s[k][k]
        for i in range(k + 1, PANEL):
            low[i, k] = s[k][i] * scale[k]
            for j in range(i, PANEL):
                s[i][j] = s[i][j] - low[i, k] * s[k][j]
            rows[i] = rows[i] - low[i, k] * rows[k]
    for k in range(PANEL - 1, -1, -1):
        rows[k] = rows[k] * scale[k]
        for i in range(k):
            pass
    for k in range(PANEL - 1, 0, -1):
        for i in range(k):
            rows[i] = rows[i] - low[k, i] * rows[k]
    solved = rows[0]
    for i in range(1, PANEL):
        solved = jnp.where(subs == i, rows[i], solved)
    pieces = []
    for g in range(1, size // PANEL):
        at = slice(g * PANEL, (g + 1) * PANEL)
        rest = jnp.where(lanes < PANEL, 0.0, a[at])
        first = cols[0][at] * rows[0]
        second = cols[1][at] * rows[1]
        for i in range(2, PANEL, 2):
            first = first + cols[i][at] * rows[i]
            second = second + cols[i + 1][at] * rows[i + 1]
        pieces.append(rest - (first + second))
    pieces.append(solved)
    return pltpu.roll(jnp.concatenate(pieces, axis=0), size - PANEL, axis=1)


def inverse_kernel(at_ref, own_ref, other_ref, zown_ref, zother_ref, s_ref, tile_ref):
    half = own_ref.shape[0]
    size = s_ref.shape[0]
    own_at = pl.ds(pl.multiple_of(at_ref[0] * half, half), half)
    other_at = pl.ds(pl.multiple_of((1 - at_ref[0]) * half, half), half)
    s_ref[own_at, :] = own_ref[...]
    s_ref[other_at, :] = other_ref[...]
    for k in range(0, size, TILE):
        at = slice(k, k + TILE)
        tile_ref[...] = s_ref[at, at]

        @pl.loop(0, TILE // PANEL)
        def _(_step):
            tile_ref[...] = panel_step(tile_ref[...])

        inverse = tile_ref[...]
        row = dot6(inverse, s_ref[at, :])
        s_ref[at, :] = row
        s_ref[at, at] = inverse
        for r in range(0, size, TILE):
            if r != k:
                rat = slice(r, r + TILE)
                column = s_ref[rat, at]
                s_ref[rat, at] = jnp.zeros((TILE, TILE), F32)
                s_ref[rat, :] = s_ref[rat, :] - dot6(column, s_ref[at, :])
    zown_ref[...] = s_ref[own_at, :]
    zother_ref[...] = s_ref[other_at, :]


SMEM = pl.BlockSpec(memory_space=pltpu.SMEM)
VMEM = pl.BlockSpec(memory_space=pltpu.VMEM)


def call(kernel, marks, operands, outs, scratch, flops, name):
    moved = 4 * sum(x.size for x in operands)
    return pl.pallas_call(
        kernel,
        out_shape=[jax.ShapeDtypeStruct(shape, F32) for shape in outs],
        in_specs=[SMEM] + [VMEM] * len(operands),
        out_specs=[VMEM] * len(outs),
        scratch_shapes=[pltpu.VMEM(shape, F32) for shape in scratch],
        cost_estimate=pl.CostEstimate(flops=flops, bytes_accessed=moved, transcendentals=0),
        compiler_params=pltpu.CompilerParams(vmem_limit_bytes=40 * 2**20),
        name=name,
    )(marks, *operands)


def inverse(marks, own, other):
    half, size = own.shape
    return call(
        inverse_kernel, marks, (own, other), [(half, size)] * 2,
        [(size, size), (TILE, TILE)], 40 * size**3, "inverse",
    )


def assemble(at_ref, own_ref, other_ref, full_ref):
    half = own_ref.shape[0]
    full_ref[pl.ds(pl.multiple_of(at_ref[0] * half, half), half), :] = own_ref[...]
    full_ref[pl.ds(pl.multiple_of((1 - at_ref[0]) * half, half), half), :] = other_ref[...]


def left_kernel(
    at_ref, zown_ref, zother_ref, u_ref, uother_ref, f_ref, d_ref, s_ref, dout_ref, sout_ref, z_ref
):
    half = u_ref.shape[0]
    assemble(at_ref, zown_ref, zother_ref, z_ref)
    z = split(z_ref[...])
    own = split(u_ref[...])
    other = split(uother_ref[...])
    inner = ((1,), (0,))
    outer = ((1,), (1,))
    own_at = pl.ds(pl.multiple_of(at_ref[0] * half, half), half)
    other_at = pl.ds(pl.multiple_of((1 - at_ref[0]) * half, half), half)
    for values, base_ref, out_ref in ((own, d_ref, dout_ref), (split(f_ref[...]), s_ref, sout_ref)):
        scaled = split(dot_parts(values, z, inner))
        out_ref[:, own_at] = base_ref[:, own_at] - dot_parts(scaled, own, outer)
        out_ref[:, other_at] = base_ref[:, other_at] - dot_parts(scaled, other, outer)


def right_kernel(
    at_ref, zown_ref, zother_ref, u_ref, f_ref, on_ref, onother_ref, d_ref, s_ref,
    dout_ref, uout_ref, sout_ref, z_ref, full_ref,
):
    half = u_ref.shape[0]
    assemble(at_ref, zown_ref, zother_ref, z_ref)
    assemble(at_ref, on_ref, onother_ref, full_ref)
    z = split(z_ref[...])
    onward = split(full_ref[...])
    inner = ((1,), (0,))
    own_at = pl.ds(pl.multiple_of(at_ref[0] * half, half), half)
    turned = dot_parts(split(full_ref[:, own_at]), z, ((0,), (0,)))
    dout_ref[...] = d_ref[...] - dot_parts(split(turned), onward, inner)
    solved = dot_parts(split(f_ref[...]), z, inner)
    sout_ref[...] = s_ref[...] - dot_parts(split(solved), onward, inner)
    scaled = dot_parts(split(u_ref[...]), z, inner)
    fresh = dot_parts(split(scaled), onward, inner)
    uout_ref[...] = jnp.where(at_ref[1] > 0, -fresh, on_ref[...])


def left(marks, z, zother, u, uother, f, d, s):
    half, size = u.shape
    return call(
        left_kernel, marks, (z, zother, u, uother, f, d, s), [(half, size)] * 2,
        [(size, size)], 12 * size**3, "left",
    )


def right(marks, z, zother, u, f, on, onother, d, s):
    half, size = u.shape
    return call(
        right_kernel, marks, (z, zother, u, f, on, onother, d, s), [(half, size)] * 3,
        [(size, size)] * 2, 18 * size**3, "right",
    )


def swapped(values):
    return lax.ppermute(values, "col", [(0, 1), (1, 0)])


def body(tm_size, diagonal_blocks, upper_blocks, right_sides):
    column = lax.axis_index("col")
    position = lax.axis_index("tm")

    def marks_of(flag):
        return jnp.stack([column, flag.astype(jnp.int32)]).astype(jnp.int32)

    up = [(i, i + 1) for i in range(tm_size - 1)]
    odd_up = [(i, i + 1) for i in range(1, tm_size - 1, 2)]
    odd_down = [(i, i - 1) for i in range(1, tm_size, 2)]

    def to(values, pairs):
        return lax.ppermute(values, "tm", pairs)

    d_even, d_odd = diagonal_blocks[0], diagonal_blocks[1]
    u_even, u_odd = upper_blocks[0], upper_blocks[1]
    f_even, f_odd = right_sides[0], right_sides[1]

    marks = marks_of(position > 0)
    d_other = swapped(d_odd)
    z, z_other = inverse(marks, d_odd, d_other)
    u_left, f_left = to(u_odd, up), to(f_odd, up)
    u_odd_other, u_even_other = swapped(u_odd), swapped(u_even)
    z_left = to(z, up)
    d, s = left(marks, z, z_other, u_odd, u_odd_other, f_odd, d_even, f_even)
    d, u, s = right(
        marks, z_left, swapped(z_left), u_left, f_left, u_even, u_even_other, d, s
    )

    marks = marks_of(jnp.logical_and(position > 0, position % 2 == 0))
    d_other = swapped(d)
    z, _ = inverse(marks, d, d_other)
    u_other = swapped(u)
    u_above, f_above = to(u, odd_down), to(s, odd_down)
    u_above_other = swapped(u_above)
    u_left, f_left = to(u, odd_up), to(s, odd_up)
    z_above, z_left = to(z, odd_down), to(z, odd_up)
    d, s2 = left(marks, z_above, swapped(z_above), u_above, u_above_other, f_above, d, s)
    d, u, s2 = right(marks, z_left, swapped(z_left), u_left, f_left, u, u_other, d, s2)
    return jnp.stack([d, d_odd]), jnp.stack([u, u_odd]), jnp.stack([s2, f_odd])


def solution(mesh):
    placed = (P("tm", "col", None),) * 3
    return jax.shard_map(
        functools.partial(body, mesh.shape["tm"]),
        mesh=mesh,
        in_specs=placed,
        out_specs=placed,
        check_vma=False,
    )
```

profile of v0, /device:TPU:12, one launch (start us, length us, event | category | flops | bytes accessed | tf_op | source)
XLA Modules:
  0.0 196.9 jit_solution(14226203598646464257)
XLA Ops:
  0.6 1.4 slice_bitcast_fusion.1
  2.0 0.1 collective-permute-start
  2.1 0.1 pad_add_fusion.1.at_ref
  2.2 1.8 collective-permute-done.other_ref
  4.0 31.0 %inverse.2 = (f32[256,512]{1,0:T(8,128)S(1)}, f32[256,512]{1,0:T(8,128)S(1)}) custom-call(s32[2]{0:T(128)S(1)} %pad_add_fusion.1.at_ref, f32[256,512]{1,0:T(8,128)S(1)} %get-tuple-element.36.own_ref, f32[256,512]{1,0:T(8,128)S(1)} %collective-permute-done.other_ref), custom_call_target="tpu_custom_call" | custom-call | flops 5368709120 | bytes 1048576 | tf_op jit(solution)/shard_map/inverse/pallas_call | solution.py:122
  35.0 0.0 copy-start.2
  35.1 3.5 %collective-permute-start.1 = (f32[256,512]{1,0:T(8,128)S(1)}, f32[256,512]{1,0:T(8,128)S(1)}, u32[]{:S(2)}, u32[]{:S(2)}) collective-permute-start(f32[256,512]{1,0:T(8,128)S(1)} %get-tuple-element.16.zown_ref), channel_id=1, source_target_pairs={{0,2},{2,4},{4,6},{6,8},{8,10},{10,12},{12,14},{14,16},{16,18},{18... | collective-permute-start | bytes 1572872 | tf_op jit(solution)/shard_map/ppermute | solution.py:218
  38.6 0.9 fusion.1
  39.6 0.0 collective-permute-start.6
  39.6 3.4 %collective-permute-start.3 = (f32[256,512]{1,0:T(8,128)S(1)}, f32[256,512]{1,0:T(8,128)S(1)}, u32[]{:S(2)}, u32[]{:S(2)}) collective-permute-start(f32[256,512]{1,0:T(8,128)S(1)} %get-tuple-element.33.u_ref), channel_id=1, source_target_pairs={{0,2},{2,4},{4,6},{6,8},{8,10},{10,12},{12,14},{14,16},{16,18},{18... | collective-permute-start | bytes 1572872 | tf_op jit(solution)/shard_map/ppermute | solution.py:218
  43.0 0.1 fusion
  43.1 3.4 %collective-permute-start.4 = (f32[256,512]{1,0:T(8,128)S(1)}, f32[256,512]{1,0:T(8,128)S(1)}, u32[]{:S(2)}, u32[]{:S(2)}) collective-permute-start(f32[256,512]{1,0:T(8,128)S(1)} %get-tuple-element.30.f_ref), channel_id=1, source_target_pairs={{0,2},{2,4},{4,6},{6,8},{8,10},{10,12},{12,14},{14,16},{16,18},{18... | collective-permute-start | bytes 1572872 | tf_op jit(solution)/shard_map/ppermute | solution.py:218
  46.5 0.1 collective-permute-start.5
  46.6 6.2 %collective-permute-done.1.zown_ref = f32[256,512]{1,0:T(8,128)S(1)} collective-permute-done((f32[256,512]{1,0:T(8,128)S(1)}, f32[256,512]{1,0:T(8,128)S(1)}, u32[]{:S(2)}, u32[]{:S(2)}) %collective-permute-start.1) | collective-permute-done | bytes 524320 | tf_op jit(solution)/shard_map/ppermute | solution.py:218
  52.8 0.0 collective-permute-start.2
  52.8 0.0 collective-permute-done.6.uother_ref
  52.8 2.7 %left.2 = (f32[256,512]{1,0:T(8,128)S(1)}, f32[256,512]{1,0:T(8,128)S(1)}) custom-call(s32[2]{0:T(128)S(1)} %pad_add_fusion.1.at_ref, f32[256,512]{1,0:T(8,128)S(1)} %get-tuple-element.16.zown_ref, f32[256,512]{1,0:T(8,128)S(1)} %get-tuple-element.17.zother_ref, f32[256,512]{1,0:T(8,128)S(1)} %get-tuple-element.33.u_ref, ...), custom_call_target="tpu_custom_call" | custom-call | flops 1610612736 | bytes 3670016 | tf_op jit(solution)/shard_map/left/pallas_call | solution.py:122
  55.5 8.5 %collective-permute-done.3.u_ref = f32[256,512]{1,0:T(8,128)S(1)} collective-permute-done((f32[256,512]{1,0:T(8,128)S(1)}, f32[256,512]{1,0:T(8,128)S(1)}, u32[]{:S(2)}, u32[]{:S(2)}) %collective-permute-start.3) | collective-permute-done | bytes 524320 | tf_op jit(solution)/shard_map/ppermute | solution.py:218
  64.0 10.4 %collective-permute-done.4.f_ref = f32[256,512]{1,0:T(8,128)S(1)} collective-permute-done((f32[256,512]{1,0:T(8,128)S(1)}, f32[256,512]{1,0:T(8,128)S(1)}, u32[]{:S(2)}, u32[]{:S(2)}) %collective-permute-start.4) | collective-permute-done | bytes 524320 | tf_op jit(solution)/shard_map/ppermute | solution.py:218
  74.4 3.6 %right.2 = (f32[256,512]{1,0:T(8,128)S(1)}, f32[256,512]{1,0:T(8,128)S(1)}, f32[256,512]{1,0:T(8,128)S(1)}) custom-call(s32[2]{0:T(128)S(1)} %pad_add_fusion.1.at_ref, f32[256,512]{1,0:T(8,128)S(1)} %collective-permute-done.1.zown_ref, f32[256,512]{1,0:T(8,128)S(1)} %collective-permute-done.2.zother_ref, f32[256,512]{1,0:T(8,128)S(1)} %collective-permute-done.3.u_ref, ...), custom_call_target="tpu_custom_call" | custom-call | flops 2415919104 | bytes 4194304 | tf_op jit(solution)/shard_map/right/pallas_call | solution.py:122
  78.1 0.1 collective-permute-start.7
  78.2 0.1 pad_add_fusion.at_ref
  78.2 1.5 collective-permute-start.15
  79.7 0.3 collective-permute-done.7.other_ref
  80.0 31.8 %inverse.3 = (f32[256,512]{1,0:T(8,128)S(1)}, f32[256,512]{1,0:T(8,128)}) custom-call(s32[2]{0:T(128)S(1)} %pad_add_fusion.at_ref, f32[256,512]{1,0:T(8,128)S(1)} %get-tuple-element.20.own_ref.d_ref, f32[256,512]{1,0:T(8,128)S(1)} %collective-permute-done.7.other_ref), custom_call_target="tpu_custom_call" | custom-call | flops 5368709120 | bytes 1048576 | tf_op jit(solution)/shard_map/inverse/pallas_call | solution.py:122
  111.9 1.3 collective-permute-start.13
  113.1 1.3 collective-permute-start.17
  114.4 0.0 collective-permute-done.15.u_ref
  114.5 0.2 collective-permute-start.16
  114.7 1.3 collective-permute-start.8
  116.0 46.3 %collective-permute-done.13.zown_ref = f32[256,512]{1,0:T(8,128)S(1)} collective-permute-done((f32[256,512]{1,0:T(8,128)S(1)}, f32[256,512]{1,0:T(8,128)S(1)}, u32[]{:S(2)}, u32[]{:S(2)}) %collective-permute-start.13) | collective-permute-done | bytes 524320 | tf_op jit(solution)/shard_map/ppermute | solution.py:218
  162.2 1.3 collective-permute-start.10
  163.5 9.2 %collective-permute-done.17.f_ref = f32[256,512]{1,0:T(8,128)S(1)} collective-permute-done((f32[256,512]{1,0:T(8,128)S(1)}, f32[256,512]{1,0:T(8,128)S(1)}, u32[]{:S(2)}, u32[]{:S(2)}) %collective-permute-start.17) | collective-permute-done | bytes 524320 | tf_op jit(solution)/shard_map/ppermute | solution.py:218
  172.7 1.3 collective-permute-start.11
  174.0 0.1 collective-permute-start.12
  174.1 0.0 collective-permute-done.8.zown_ref
  174.1 0.5 collective-permute-start.9
  174.6 0.0 collective-permute-done.14.zother_ref
  174.6 2.7 %left.3 = (f32[256,512]{1,0:T(8,128)S(1)}, f32[256,512]{1,0:T(8,128)S(1)}) custom-call(s32[2]{0:T(128)S(1)} %pad_add_fusion.at_ref, f32[256,512]{1,0:T(8,128)S(1)} %collective-permute-done.13.zown_ref, f32[256,512]{1,0:T(8,128)S(1)} %collective-permute-done.14.zother_ref, f32[256,512]{1,0:T(8,128)S(1)} %collective-permute-done.15.u_ref, ...), custom_call_target="tpu_custom_call" | custom-call | flops 1610612736 | bytes 3670016 | tf_op jit(solution)/shard_map/left/pallas_call | solution.py:122
  177.3 2.6 %collective-permute-done.10.u_ref = f32[256,512]{1,0:T(8,128)S(1)} collective-permute-done((f32[256,512]{1,0:T(8,128)S(1)}, f32[256,512]{1,0:T(8,128)S(1)}, u32[]{:S(2)}, u32[]{:S(2)}) %collective-permute-start.10) | collective-permute-done | bytes 524320 | tf_op jit(solution)/shard_map/ppermute | solution.py:218
  179.8 10.8 %collective-permute-done.11.f_ref = f32[256,512]{1,0:T(8,128)S(1)} collective-permute-done((f32[256,512]{1,0:T(8,128)S(1)}, f32[256,512]{1,0:T(8,128)S(1)}, u32[]{:S(2)}, u32[]{:S(2)}) %collective-permute-start.11) | collective-permute-done | bytes 524320 | tf_op jit(solution)/shard_map/ppermute | solution.py:218
  190.6 0.0 collective-permute-done.12.onother_ref
  190.6 0.0 collective-permute-done.9.zother_ref
  190.6 3.6 %right.3 = (f32[256,512]{1,0:T(8,128)S(1)}, f32[256,512]{1,0:T(8,128)S(1)}, f32[256,512]{1,0:T(8,128)S(1)}) custom-call(s32[2]{0:T(128)S(1)} %pad_add_fusion.at_ref, f32[256,512]{1,0:T(8,128)S(1)} %collective-permute-done.8.zown_ref, f32[256,512]{1,0:T(8,128)S(1)} %collective-permute-done.9.zother_ref, f32[256,512]{1,0:T(8,128)S(1)} %collective-permute-done.10.u_ref, ...), custom_call_target="tpu_custom_call" | custom-call | flops 2415919104 | bytes 4194304 | tf_op jit(solution)/shard_map/right/pallas_call | solution.py:122
  194.2 0.0 copy-start
  194.2 1.1 pad_maximum_fusion.2
  195.3 0.0 copy-done
  195.3 1.5 pad_maximum_fusion
  (7 shorter events, 0.0 us)
Async XLA Ops:
  2.0 2.0 %collective-permute-start = (f32[256,512]{1,0:T(8,128)S(1)}, f32[256,512]{1,0:T(8,128)S(1)}, u32[]{:S(2)}, u32[]{:S(2)}) collective-permute-start(f32[256,512]{1,0:T(8,128)S(1)} %get-tuple-element.36.own_ref), channel_id=1, source_target_pairs={{0,1},{1,0},{2,3},{3,2},{4,5},{5,4},{6,7},{7,6},{8,9},{9,8},{10,11... | collective-permute-start | bytes 1572872 | tf_op jit(solution)/shard_map/ppermute | solution.py:203
  2.2 36.4 %copy-start.1 = (f32[2,256,512]{2,1,0:T(8,128)S(1)}, f32[2,256,512]{2,1,0:T(8,128)}, u32[]{:S(2)}) copy-start(f32[2,256,512]{2,1,0:T(8,128)} %param.4) | copy-start | bytes 3145732
  35.0 7.9 %copy-start.2 = (f32[2,256,512]{2,1,0:T(8,128)S(1)}, f32[2,256,512]{2,1,0:T(8,128)}, u32[]{:S(2)}) copy-start(f32[2,256,512]{2,1,0:T(8,128)} %param.5) | copy-start | bytes 3145732
  35.1 17.7 %collective-permute-start.1 = (f32[256,512]{1,0:T(8,128)S(1)}, f32[256,512]{1,0:T(8,128)S(1)}, u32[]{:S(2)}, u32[]{:S(2)}) collective-permute-start(f32[256,512]{1,0:T(8,128)S(1)} %get-tuple-element.16.zown_ref), channel_id=1, source_target_pairs={{0,2},{2,4},{4,6},{6,8},{8,10},{10,12},{12,14},{14,16},{16,18},{18... | collective-permute-start | bytes 1572872 | tf_op jit(solution)/shard_map/ppermute | solution.py:218
  39.6 13.2 %collective-permute-start.6 = (f32[256,512]{1,0:T(8,128)S(1)}, f32[256,512]{1,0:T(8,128)S(1)}, u32[]{:S(2)}, u32[]{:S(2)}) collective-permute-start(f32[256,512]{1,0:T(8,128)S(1)} %get-tuple-element.33.u_ref), channel_id=1, source_target_pairs={{0,1},{1,0},{2,3},{3,2},{4,5},{5,4},{6,7},{7,6},{8,9},{9,8},{10,11... | collective-permute-start | bytes 1572872 | tf_op jit(solution)/shard_map/ppermute | solution.py:203
  39.6 24.5 %collective-permute-start.3 = (f32[256,512]{1,0:T(8,128)S(1)}, f32[256,512]{1,0:T(8,128)S(1)}, u32[]{:S(2)}, u32[]{:S(2)}) collective-permute-start(f32[256,512]{1,0:T(8,128)S(1)} %get-tuple-element.33.u_ref), channel_id=1, source_target_pairs={{0,2},{2,4},{4,6},{6,8},{8,10},{10,12},{12,14},{14,16},{16,18},{18... | collective-permute-start | bytes 1572872 | tf_op jit(solution)/shard_map/ppermute | solution.py:218
  43.1 31.3 %collective-permute-start.4 = (f32[256,512]{1,0:T(8,128)S(1)}, f32[256,512]{1,0:T(8,128)S(1)}, u32[]{:S(2)}, u32[]{:S(2)}) collective-permute-start(f32[256,512]{1,0:T(8,128)S(1)} %get-tuple-element.30.f_ref), channel_id=1, source_target_pairs={{0,2},{2,4},{4,6},{6,8},{8,10},{10,12},{12,14},{14,16},{16,18},{18... | collective-permute-start | bytes 1572872 | tf_op jit(solution)/shard_map/ppermute | solution.py:218
  46.5 27.9 %collective-permute-start.5 = (f32[256,512]{1,0:T(8,128)S(1)}, f32[256,512]{1,0:T(8,128)S(1)}, u32[]{:S(2)}, u32[]{:S(2)}) collective-permute-start(f32[256,512]{1,0:T(8,128)S(1)} %get-tuple-element.34.on_ref), channel_id=1, source_target_pairs={{0,1},{1,0},{2,3},{3,2},{4,5},{5,4},{6,7},{7,6},{8,9},{9,8},{10,11... | collective-permute-start | bytes 1572872 | tf_op jit(solution)/shard_map/ppermute | solution.py:203
  52.8 21.6 %collective-permute-start.2 = (f32[256,512]{1,0:T(8,128)S(1)}, f32[256,512]{1,0:T(8,128)S(1)}, u32[]{:S(2)}, u32[]{:S(2)}) collective-permute-start(f32[256,512]{1,0:T(8,128)S(1)} %collective-permute-done.1.zown_ref), channel_id=1, source_target_pairs={{0,1},{1,0},{2,3},{3,2},{4,5},{5,4},{6,7},{7,6},{8,9},{9,8},{10,11... | collective-permute-start | bytes 1572872 | tf_op jit(solution)/shard_map/ppermute | solution.py:203
  78.1 2.0 %collective-permute-start.7 = (f32[256,512]{1,0:T(8,128)S(1)}, f32[256,512]{1,0:T(8,128)S(1)}, u32[]{:S(2)}, u32[]{:S(2)}) collective-permute-start(f32[256,512]{1,0:T(8,128)S(1)} %get-tuple-element.20.own_ref.d_ref), channel_id=1, source_target_pairs={{0,1},{1,0},{2,3},{3,2},{4,5},{5,4},{6,7},{7,6},{8,9},{9,8},{10,11... | collective-permute-start | bytes 1572872 | tf_op jit(solution)/shard_map/ppermute | solution.py:203
  78.2 36.2 %collective-permute-start.15 = (f32[256,512]{1,0:T(8,128)S(1)}, f32[256,512]{1,0:T(8,128)S(1)}, u32[]{:S(2)}, u32[]{:S(2)}) collective-permute-start(f32[256,512]{1,0:T(8,128)S(1)} %get-tuple-element.22.on_ref), channel_id=1, source_target_pairs={{2,0},{6,4},{10,8},{14,12},{18,16},{22,20},{26,24},{30,28},{3,1},{... | collective-permute-start | bytes 1572872 | tf_op jit(solution)/shard_map/ppermute | solution.py:218
  111.9 50.4 %collective-permute-start.13 = (f32[256,512]{1,0:T(8,128)S(1)}, f32[256,512]{1,0:T(8,128)S(1)}, u32[]{:S(2)}, u32[]{:S(2)}) collective-permute-start(f32[256,512]{1,0:T(8,128)S(1)} %get-tuple-element.21), channel_id=1, source_target_pairs={{2,0},{6,4},{10,8},{14,12},{18,16},{22,20},{26,24},{30,28},{3,1},{... | collective-permute-start | bytes 1572872 | tf_op jit(solution)/shard_map/ppermute | solution.py:218
  113.1 59.6 %collective-permute-start.17 = (f32[256,512]{1,0:T(8,128)S(1)}, f32[256,512]{1,0:T(8,128)S(1)}, u32[]{:S(2)}, u32[]{:S(2)}) collective-permute-start(f32[256,512]{1,0:T(8,128)S(1)} %get-tuple-element.23.s_ref), channel_id=1, source_target_pairs={{2,0},{6,4},{10,8},{14,12},{18,16},{22,20},{26,24},{30,28},{3,1},{... | collective-permute-start | bytes 1572872 | tf_op jit(solution)/shard_map/ppermute | solution.py:218
  114.5 59.5 %collective-permute-start.16 = (f32[256,512]{1,0:T(8,128)S(1)}, f32[256,512]{1,0:T(8,128)S(1)}, u32[]{:S(2)}, u32[]{:S(2)}) collective-permute-start(f32[256,512]{1,0:T(8,128)S(1)} %collective-permute-done.15.u_ref), channel_id=1, source_target_pairs={{0,1},{1,0},{2,3},{3,2},{4,5},{5,4},{6,7},{7,6},{8,9},{9,8},{10,11... | collective-permute-start | bytes 1572872 | tf_op jit(solution)/shard_map/ppermute | solution.py:203
  114.7 59.4 %collective-permute-start.8 = (f32[256,512]{1,0:T(8,128)S(1)}, f32[256,512]{1,0:T(8,128)S(1)}, u32[]{:S(2)}, u32[]{:S(2)}) collective-permute-start(f32[256,512]{1,0:T(8,128)S(1)} %get-tuple-element.21), channel_id=1, source_target_pairs={{2,4},{6,8},{10,12},{14,16},{18,20},{22,24},{26,28},{3,5},{7,9},{1... | collective-permute-start | bytes 1572872 | tf_op jit(solution)/shard_map/ppermute | solution.py:218
  162.2 12.3 %collective-permute-start.14 = (f32[256,512]{1,0:T(8,128)S(1)}, f32[256,512]{1,0:T(8,128)S(1)}, u32[]{:S(2)}, u32[]{:S(2)}) collective-permute-start(f32[256,512]{1,0:T(8,128)S(1)} %collective-permute-done.13.zown_ref), channel_id=1, source_target_pairs={{0,1},{1,0},{2,3},{3,2},{4,5},{5,4},{6,7},{7,6},{8,9},{9,8},{10,11... | collective-permute-start | bytes 1572872 | tf_op jit(solution)/shard_map/ppermute | solution.py:203
  162.2 17.6 %collective-permute-start.10 = (f32[256,512]{1,0:T(8,128)S(1)}, f32[256,512]{1,0:T(8,128)S(1)}, u32[]{:S(2)}, u32[]{:S(2)}) collective-permute-start(f32[256,512]{1,0:T(8,128)S(1)} %get-tuple-element.22.on_ref), channel_id=1, source_target_pairs={{2,4},{6,8},{10,12},{14,16},{18,20},{22,24},{26,28},{3,5},{7,9},{1... | collective-permute-start | bytes 1572872 | tf_op jit(solution)/shard_map/ppermute | solution.py:218
  172.7 17.9 %collective-permute-start.11 = (f32[256,512]{1,0:T(8,128)S(1)}, f32[256,512]{1,0:T(8,128)S(1)}, u32[]{:S(2)}, u32[]{:S(2)}) collective-permute-start(f32[256,512]{1,0:T(8,128)S(1)} %get-tuple-element.23.s_ref), channel_id=1, source_target_pairs={{2,4},{6,8},{10,12},{14,16},{18,20},{22,24},{26,28},{3,5},{7,9},{1... | collective-permute-start | bytes 1572872 | tf_op jit(solution)/shard_map/ppermute | solution.py:218
  174.0 16.6 %collective-permute-start.12 = (f32[256,512]{1,0:T(8,128)S(1)}, f32[256,512]{1,0:T(8,128)S(1)}, u32[]{:S(2)}, u32[]{:S(2)}) collective-permute-start(f32[256,512]{1,0:T(8,128)S(1)} %get-tuple-element.22.on_ref), channel_id=1, source_target_pairs={{0,1},{1,0},{2,3},{3,2},{4,5},{5,4},{6,7},{7,6},{8,9},{9,8},{10,11... | collective-permute-start | bytes 1572872 | tf_op jit(solution)/shard_map/ppermute | solution.py:203
  174.1 16.5 %collective-permute-start.9 = (f32[256,512]{1,0:T(8,128)S(1)}, f32[256,512]{1,0:T(8,128)S(1)}, u32[]{:S(2)}, u32[]{:S(2)}) collective-permute-start(f32[256,512]{1,0:T(8,128)S(1)} %collective-permute-done.8.zown_ref), channel_id=1, source_target_pairs={{0,1},{1,0},{2,3},{3,2},{4,5},{5,4},{6,7},{7,6},{8,9},{9,8},{10,11... | collective-permute-start | bytes 1572872 | tf_op jit(solution)/shard_map/ppermute | solution.py:203
  194.2 1.1 copy-start
where the time goes:
time: 197 us
  waiting for transfers between devices  96.1 us (49%)
  Pallas kernels  75.4 us (38%)
  starting transfers between devices  19.2 us (10%)
  other arithmetic  2.74 us (1%)
  local copies, waits for them, and re-layouts  2.53 us (1%)
    ppermute x9, waiting for transfers between devices, to(): return lax.ppermute(values, 'tm', pairs)  93.9 us
    pallas_call x6, Pallas kernels, call(): pl.pallas_call(kernel, out_shape=[jax.ShapeDtypeStruct(shape, F32) for sh...  75.4 us
    ppermute x9, starting transfers between devices, to(): return lax.ppermute(values, 'tm', pairs)  18.2 us
  transfers between devices with their start and end apart: 18, of which 9 were waited for; matrix products, arithmetic and copies ran while one was open for 1% of the time, Pallas kernels for 19%

commit v1 on v0

v1 whole, which is shorter than its diff:
```python
import functools

import jax
import jax.numpy as jnp
from jax import lax
from jax.experimental import pallas as pl
from jax.experimental.pallas import tpu as pltpu
from jax.sharding import PartitionSpec as P

LEVELS = 2
TILE = 128
PANEL = 8
F32 = jnp.float32
BF16 = jnp.bfloat16


def split(values):
    high = values.astype(BF16)
    return high, (values - high.astype(F32)).astype(BF16)


def dot_parts(left, right, dims):
    def one(a, b):
        return lax.dot_general(a, b, (dims, ((), ())), preferred_element_type=F32)

    return one(left[0], right[0]) + (one(left[0], right[1]) + one(left[1], right[0]))


def dot3(left, right, dims=((1,), (0,))):
    return dot_parts(split(left), split(right), dims)


def dot6(left, right):
    return jnp.dot(left, right, precision=lax.Precision.HIGHEST, preferred_element_type=F32)


def panel_step(a):
    size = a.shape[0]
    lanes = lax.broadcasted_iota(jnp.int32, (PANEL, size), 1)
    subs = lax.broadcasted_iota(jnp.int32, (PANEL, size), 0)
    cols = [jnp.broadcast_to(a[:, i : i + 1], (size, size)) for i in range(PANEL)]
    rows = [
        jnp.where(
            lanes < PANEL,
            jnp.where(lanes == i, 1.0, 0.0),
            jnp.broadcast_to(a[i : i + 1, :], (PANEL, size)),
        )
        for i in range(PANEL)
    ]
    s = [
        [jnp.broadcast_to(cols[j][i : i + 1, :], (PANEL, size)) if j >= i else None for j in range(PANEL)]
        for i in range(PANEL)
    ]
    scale = [None] * PANEL
    low = {}
    for k in range(PANEL):
        scale[k] = 1.0 / s[k][k]
        for i in range(k + 1, PANEL):
            low[i, k] = s[k][i] * scale[k]
            for j in range(i, PANEL):
                s[i][j] = s[i][j] - low[i, k] * s[k][j]
            rows[i] = rows[i] - low[i, k] * rows[k]
    for k in range(PANEL - 1, -1, -1):
        rows[k] = rows[k] * scale[k]
        for i in range(k):
            pass
    for k in range(PANEL - 1, 0, -1):
        for i in range(k):
            rows[i] = rows[i] - low[k, i] * rows[k]
    solved = rows[0]
    for i in range(1, PANEL):
        solved = jnp.where(subs == i, rows[i], solved)
    pieces = []
    for g in range(1, size // PANEL):
        at = slice(g * PANEL, (g + 1) * PANEL)
        rest = jnp.where(lanes < PANEL, 0.0, a[at])
        first = cols[0][at] * rows[0]
        second = cols[1][at] * rows[1]
        for i in range(2, PANEL, 2):
            first = first + cols[i][at] * rows[i]
            second = second + cols[i + 1][at] * rows[i + 1]
        pieces.append(rest - (first + second))
    pieces.append(solved)
    return pltpu.roll(jnp.concatenate(pieces, axis=0), size - PANEL, axis=1)


INNER = ((1,), (0,))
OUTER = ((1,), (1,))
CHUNKS = 2


def invert(s_ref, tile_ref):
    size = s_ref.shape[0]
    for k in range(0, size, TILE):
        at = slice(k, k + TILE)
        tile_ref[...] = s_ref[at, at]

        @pl.loop(0, TILE // PANEL)
        def _(_step):
            tile_ref[...] = panel_step(tile_ref[...])

        inverse = tile_ref[...]
        row = dot6(inverse, s_ref[at, :])
        s_ref[at, :] = row
        s_ref[at, at] = inverse
        for r in range(0, size, TILE):
            if r != k:
                rat = slice(r, r + TILE)
                column = s_ref[rat, at]
                s_ref[rat, at] = jnp.zeros((TILE, TILE), F32)
                s_ref[rat, :] = s_ref[rat, :] - dot6(column, s_ref[at, :])


def kernel(
    tm_size, d_ref, u_ref, f_ref, dout_ref, uout_ref, fout_ref,
    s_ref, tile_ref, z_ref, full_ref, zown, cur, bufs, send_sem, recv_sem,
):
    half, size = d_ref.shape[1], d_ref.shape[2]
    column = lax.axis_index("col")
    place = lax.axis_index("tm")
    above, below = lax.rem(place + 1, tm_size), lax.rem(place + tm_size - 1, tm_size)
    partner = 1 - column
    odd = lax.rem(place, 2) == 1
    even = lax.rem(place, 2) == 0
    has_left = place > 0
    has_right = place < tm_size - 1
    odd_right = jnp.logical_and(odd, has_right)
    even_left = jnp.logical_and(even, has_left)
    own_at = pl.ds(pl.multiple_of(column * half, half), half)
    other_at = pl.ds(pl.multiple_of(partner * half, half), half)
    rows = half // CHUNKS

    barrier = pltpu.get_barrier_semaphore()

    def greet(where):
        pl.semaphore_signal(barrier, inc=1, device_id=where, device_id_type=pl.DeviceIdType.MESH)

    greet((place, partner))
    pl.when(has_left)(lambda: greet((below, column)))
    pl.when(has_right)(lambda: greet((above, column)))
    pl.semaphore_wait(barrier, 1 + has_left.astype(jnp.int32) + has_right.astype(jnp.int32))

    targets = {"above": (above, column), "below": (below, column), "partner": (place, partner)}

    def copy(slot, source, target, chunk=None):
        sem = CHUNKS * slot + (chunk or 0)
        if chunk is not None:
            at = slice(chunk * rows, (chunk + 1) * rows)
            source, landing = source.at[at], bufs.at[slot, at]
        else:
            landing = bufs.at[slot]
        return pltpu.make_async_remote_copy(
            src_ref=source, dst_ref=landing, send_sem=send_sem.at[sem], recv_sem=recv_sem.at[sem],
            device_id=targets[target], device_id_type=pl.DeviceIdType.MESH,
        )

    def assemble(into, own, other):
        into[own_at, :] = own[...]
        into[other_at, :] = other[...]

    def left(u, uother, f, d, s, dto, sto):
        z = split(z_ref[...])
        own, other = split(u[...]), split(uother[...])
        for values, base, out in ((own, d, dto), (split(f[...]), s, sto)):
            scaled = split(dot_parts(values, z, INNER))
            out[:, own_at] = base[:, own_at] - dot_parts(scaled, own, OUTER)
            out[:, other_at] = base[:, other_at] - dot_parts(scaled, other, OUTER)

    def right(u, f, dto, uto, sto):
        z = split(z_ref[...])
        onward = split(full_ref[...])
        turned = dot_parts(split(full_ref[:, own_at]), z, ((0,), (0,)))
        dto[...] = dto[...] - dot_parts(split(turned), onward, INNER)
        solved = dot_parts(split(f[...]), z, INNER)
        sto[...] = sto[...] - dot_parts(split(solved), onward, INNER)
        scaled = dot_parts(split(u[...]), z, INNER)
        uto[...] = -dot_parts(split(scaled), onward, INNER)

    c_do = copy(0, d_ref.at[1], "partner")
    c_uo = copy(1, u_ref.at[1], "partner")
    c_eo = copy(2, u_ref.at[0], "partner")
    c_ul = copy(3, u_ref.at[1], "above")
    c_fl = copy(4, f_ref.at[1], "above")
    c_zl = [copy(5, zown.at[0], "above", i) for i in range(CHUNKS)]
    c_zlo = [copy(6, bufs.at[5], "partner", i) for i in range(CHUNKS)]
    c_do.start()

    @pl.when(has_right)
    def _():
        c_ul.start()
        c_fl.start()

    c_uo.start()
    c_eo.start()
    c_do.wait_recv()
    assemble(s_ref, d_ref.at[1], bufs.at[0])
    invert(s_ref, tile_ref)
    zown[0] = s_ref[own_at, :]

    @pl.when(has_right)
    def _():
        for i in c_zl:
            i.start()

    c_uo.wait_recv()
    z_ref[...] = s_ref[...]
    left(u_ref.at[1], bufs.at[1], f_ref.at[1], d_ref.at[0], f_ref.at[0], cur.at[0], cur.at[2])
    c_eo.wait_recv()
    cur[1] = u_ref[0]

    @pl.when(has_left)
    def _():
        assemble(full_ref, u_ref.at[0], bufs.at[2])
        c_ul.wait_recv()
        c_fl.wait_recv()
        for i in range(CHUNKS):
            c_zl[i].wait_recv()
            c_zlo[i].start()
        for i in range(CHUNKS):
            c_zlo[i].wait_recv()
        assemble(z_ref, bufs.at[5], bufs.at[6])
        right(bufs.at[3], bufs.at[4], cur.at[0], cur.at[1], cur.at[2])

    c_do1 = copy(7, cur.at[0], "partner")
    c_uo1 = copy(8, cur.at[1], "partner")
    c_ua = copy(9, cur.at[1], "below")
    c_fa = copy(10, cur.at[2], "below")
    c_uao = copy(11, bufs.at[9], "partner")
    c_za = [copy(12, zown.at[1], "below", i) for i in range(CHUNKS)]
    c_zao = [copy(13, bufs.at[12], "partner", i) for i in range(CHUNKS)]
    c_ul1 = copy(14, cur.at[1], "above")
    c_fl1 = copy(15, cur.at[2], "above")
    c_zl1 = [copy(16, zown.at[1], "above", i) for i in range(CHUNKS)]
    c_zl1o = [copy(17, bufs.at[16], "partner", i) for i in range(CHUNKS)]

    @pl.when(odd)
    def _():
        c_do1.start()
        c_ua.start()
        c_fa.start()

        @pl.when(has_right)
        def _():
            c_ul1.start()
            c_fl1.start()

        c_do1.wait_recv()
        assemble(s_ref, cur.at[0], bufs.at[7])
        invert(s_ref, tile_ref)
        zown[1] = s_ref[own_at, :]
        for i in c_za:
            i.start()

        @pl.when(has_right)
        def _():
            for i in c_zl1:
                i.start()

        dout_ref[0] = cur[0]
        uout_ref[0] = cur[1]
        fout_ref[0] = cur[2]

    dout_ref[1] = d_ref[1]
    uout_ref[1] = u_ref[1]
    fout_ref[1] = f_ref[1]

    @pl.when(even)
    def _():
        c_uo1.start()
        c_ua.wait_recv()
        c_uao.start()
        c_uo1.wait_recv()
        assemble(full_ref, cur.at[1], bufs.at[8])
        uout_ref[0] = cur[1]
        c_fa.wait_recv()
        c_uao.wait_recv()
        for i in range(CHUNKS):
            c_za[i].wait_recv()
            c_zao[i].start()
        for i in range(CHUNKS):
            c_zao[i].wait_recv()
        assemble(z_ref, bufs.at[12], bufs.at[13])
        left(bufs.at[9], bufs.at[11], bufs.at[10], cur.at[0], cur.at[2], dout_ref.at[0], fout_ref.at[0])

    @pl.when(even_left)
    def _():
        c_ul1.wait_recv()
        c_fl1.wait_recv()
        for i in range(CHUNKS):
            c_zl1[i].wait_recv()
            c_zl1o[i].start()
        for i in range(CHUNKS):
            c_zl1o[i].wait_recv()
        assemble(z_ref, bufs.at[16], bufs.at[17])
        right(bufs.at[14], bufs.at[15], dout_ref.at[0], uout_ref.at[0], fout_ref.at[0])

    def drained(condition, copies):
        @pl.when(condition)
        def _():
            for i in copies:
                i.wait_send()

    for i in (c_do, c_uo, c_eo):
        i.wait_send()
    drained(has_right, [c_ul, c_fl] + c_zl)
    drained(has_left, c_zlo)
    drained(odd, [c_do1, c_ua, c_fa] + c_za)
    drained(odd_right, [c_ul1, c_fl1] + c_zl1)
    drained(even, [c_uo1, c_uao] + c_zao)
    drained(even_left, c_zl1o)


SLOTS = 18


def body(tm_size, diagonal_blocks, upper_blocks, right_sides):
    shape = diagonal_blocks.shape
    half, size = shape[1], shape[2]
    whole = pl.BlockSpec(memory_space=pltpu.VMEM)
    return pl.pallas_call(
        functools.partial(kernel, tm_size),
        out_shape=[jax.ShapeDtypeStruct(shape, F32)] * 3,
        in_specs=[whole] * 3,
        out_specs=[whole] * 3,
        scratch_shapes=[
            pltpu.VMEM((size, size), F32),
            pltpu.VMEM((TILE, TILE), F32),
            pltpu.VMEM((size, size), F32),
            pltpu.VMEM((size, size), F32),
            pltpu.VMEM((2, half, size), F32),
            pltpu.VMEM((3, half, size), F32),
            pltpu.VMEM((SLOTS, half, size), F32),
            pltpu.SemaphoreType.DMA((SLOTS * CHUNKS,)),
            pltpu.SemaphoreType.DMA((SLOTS * CHUNKS,)),
        ],
        compiler_params=pltpu.CompilerParams(
            vmem_limit_bytes=50 * 2**20, collective_id=0, has_side_effects=True
        ),
        name="reduce_levels",
    )(diagonal_blocks, upper_blocks, right_sides)


def solution(mesh):
    placed = (P("tm", "col", None),) * 3
    return jax.shard_map(
        functools.partial(body, mesh.shape["tm"]),
        mesh=mesh,
        in_specs=placed,
        out_specs=placed,
        check_vma=False,
    )
```

time: 197 us -> 135 us (0.69)
  waiting for transfers between devices: 96.1 us -> 0 us
  Pallas kernels: 75.4 us -> 131 us
  starting transfers between devices: 19.2 us -> 0 us
  other arithmetic: 2.74 us -> 0 us
    ppermute x18 -> x0, waiting for transfers between devices: 96.1 us -> none  [the longest x9 93.9 us: to(): return lax.ppermute(values, 'tm', pairs)]
    pallas_call x6 -> x1, Pallas kernels: 75.4 us -> 131 us  [body(): pl.pallas_call(functools.partial(kernel, tm_size), out_shape=[jax.ShapeDt...]
    ppermute x18 -> x0, starting transfers between devices: 19.2 us -> none  [the longest x9 18.2 us: to(): return lax.ppermute(values, 'tm', pairs)]
    unnamed x6 -> x3, local copies, waits for them, and re-layouts: 0.05 us -> 2.91 us
    another operation x4 -> x0, other arithmetic: 2.74 us -> none  [the longest x1 1.52 us: body(): jnp.stack([d, d_odd])]
  transfers between devices with their start and end apart: 18 -> 0, of which waited for: 9 -> 0; matrix products, arithmetic and copies ran while one was open for 1% -> 0% of each run, Pallas kernels for 19% -> 0%
where the time goes in v1:
time: 135 us
  Pallas kernels  131 us (97%)
  local copies, waits for them, and re-layouts  2.91 us (2%)
    pallas_call x1, Pallas kernels, body(): pl.pallas_call(functools.partial(kernel, tm_size), out_shape=[jax.ShapeDt...  131 us
    unnamed x3, local copies, waits for them, and re-layouts  2.91 us

profile of v1, /device:TPU:12, one launch (start us, length us, event | category | flops | bytes accessed | tf_op | source)
XLA Modules:
  0.0 134.7 jit_solution(15628281503294171650)
XLA Ops:
  0.6 131.2 %reduce_levels.1 = (f32[2,256,512]{2,1,0:T(8,128)S(1)}, f32[2,256,512]{2,1,0:T(8,128)S(1)}, f32[2,256,512]{2,1,0:T(8,128)S(1)}) custom-call(f32[2,256,512]{2,1,0:T(8,128)} %d_ref.1, f32[2,256,512]{2,1,0:T(8,128)} %u_ref.1, f32[2,256,512]{2,1,0:T(8,128)} %f_ref.1), custom_call_target="tpu_custom_call" | custom-call | tf_op jit(solution)/shard_map/reduce_levels/pallas_call | solution.py:320
  131.8 1.0 copy.9
  132.8 1.0 copy.10
  133.7 1.0 copy.11

commit v2 on v1

--- a/solution.py
+++ b/solution.py
@@ -30,25 +30,28 @@
     return dot_parts(split(left), split(right), dims)
 
 
-def dot6(left, right):
-    return jnp.dot(left, right, precision=lax.Precision.HIGHEST, preferred_element_type=F32)
-
-
-def panel_step(a):
-    size = a.shape[0]
+def panel_step(a, p):
+    size = a[0].shape[1]
+    count = size // PANEL
+    base = PANEL * p
     lanes = lax.broadcasted_iota(jnp.int32, (PANEL, size), 1)
     subs = lax.broadcasted_iota(jnp.int32, (PANEL, size), 0)
-    cols = [jnp.broadcast_to(a[:, i : i + 1], (size, size)) for i in range(PANEL)]
+    inside = jnp.logical_and(lanes >= base, lanes < base + PANEL)
+
+    def spread(values, i):
+        return jnp.broadcast_to(values[:, base + i : base + i + 1], (PANEL, size))
+
+    head = [spread(a[p], i) for i in range(PANEL)]
+    s = [
+        [jnp.broadcast_to(head[j][i : i + 1, :], (PANEL, size)) if j >= i else None for j in range(PANEL)]
+        for i in range(PANEL)
+    ]
     rows = [
         jnp.where(
-            lanes < PANEL,
-            jnp.where(lanes == i, 1.0, 0.0),
-            jnp.broadcast_to(a[i : i + 1, :], (PANEL, size)),
+            inside,
+            jnp.where(lanes == base + i, 1.0, 0.0),
+            jnp.broadcast_to(a[p][i : i + 1, :], (PANEL, size)),
         )
-        for i in range(PANEL)
-    ]
-    s = [
-        [jnp.broadcast_to(cols[j][i : i + 1, :], (PANEL, size)) if j >= i else None for j in range(PANEL)]
         for i in range(PANEL)
     ]
     scale = [None] * PANEL
@@ -60,55 +63,59 @@
             for j in range(i, PANEL):
                 s[i][j] = s[i][j] - low[i, k] * s[k][j]
             rows[i] = rows[i] - low[i, k] * rows[k]
-    for k in range(PANEL - 1, -1, -1):
+    for k in range(PANEL):
         rows[k] = rows[k] * scale[k]
-        for i in range(k):
-            pass
     for k in range(PANEL - 1, 0, -1):
         for i in range(k):
             rows[i] = rows[i] - low[k, i] * rows[k]
     solved = rows[0]
     for i in range(1, PANEL):
         solved = jnp.where(subs == i, rows[i], solved)
-    pieces = []
-    for g in range(1, size // PANEL):
-        at = slice(g * PANEL, (g + 1) * PANEL)
-        rest = jnp.where(lanes < PANEL, 0.0, a[at])
-        first = cols[0][at] * rows[0]
-        second = cols[1][at] * rows[1]
-        for i in range(2, PANEL, 2):
-            first = first + cols[i][at] * rows[i]
-            second = second + cols[i + 1][at] * rows[i + 1]
-        pieces.append(rest - (first + second))
-    pieces.append(solved)
-    return pltpu.roll(jnp.concatenate(pieces, axis=0), size - PANEL, axis=1)
+    fresh = [None] * count
+    fresh[p] = solved
+    for step in range(1, count):
+        g = (p + step) % count
+        col = [spread(a[g], i) for i in range(PANEL)]
+        terms = [col[i] * rows[i] for i in range(PANEL)]
+        while len(terms) > 1:
+            terms = [terms[i] + terms[i + 1] for i in range(0, len(terms), 2)]
+        fresh[g] = jnp.where(inside, 0.0, a[g]) - terms[0]
+    return fresh
 
 
 INNER = ((1,), (0,))
 OUTER = ((1,), (1,))
-CHUNKS = 2
+CHUNKS = 4
 
 
 def invert(s_ref, tile_ref):
     size = s_ref.shape[0]
-    for k in range(0, size, TILE):
-        at = slice(k, k + TILE)
-        tile_ref[...] = s_ref[at, at]
-
-        @pl.loop(0, TILE // PANEL)
-        def _(_step):
-            tile_ref[...] = panel_step(tile_ref[...])
-
+    blocks = size // TILE
+
+    @pl.loop(0, blocks)
+    def _(k):
+        at = pl.ds(pl.multiple_of(k * TILE, TILE), TILE)
+        groups = [
+            s_ref[pl.ds(pl.multiple_of(k * TILE, TILE) + PANEL * g, PANEL), at]
+            for g in range(TILE // PANEL)
+        ]
+        for p in range(TILE // PANEL):
+            groups = panel_step(groups, p)
+        for g in range(TILE // PANEL):
+            tile_ref[PANEL * g : PANEL * (g + 1), :] = groups[g]
         inverse = tile_ref[...]
-        row = dot6(inverse, s_ref[at, :])
+        row = dot3(inverse, s_ref[at, :])
         s_ref[at, :] = row
         s_ref[at, at] = inverse
-        for r in range(0, size, TILE):
-            if r != k:
-                rat = slice(r, r + TILE)
+        row_parts = split(s_ref[at, :])
+        for r in range(blocks):
+
+            @pl.when(r != k)
+            def _():
+                rat = slice(r * TILE, (r + 1) * TILE)
                 column = s_ref[rat, at]
                 s_ref[rat, at] = jnp.zeros((TILE, TILE), F32)
-                s_ref[rat, :] = s_ref[rat, :] - dot6(column, s_ref[at, :])
+                s_ref[rat, :] = s_ref[rat, :] - dot_parts(split(column), row_parts, INNER)
 
 
 def kernel(
@@ -119,13 +126,14 @@
     column = lax.axis_index("col")
     place = lax.axis_index("tm")
     above, below = lax.rem(place + 1, tm_size), lax.rem(place + tm_size - 1, tm_size)
+    over, under = lax.rem(place + 2, tm_size), lax.rem(place + tm_size - 2, tm_size)
     partner = 1 - column
     odd = lax.rem(place, 2) == 1
     even = lax.rem(place, 2) == 0
     has_left = place > 0
     has_right = place < tm_size - 1
-    odd_right = jnp.logical_and(odd, has_right)
     even_left = jnp.logical_and(even, has_left)
+    even_right = jnp.logical_and(even, place < tm_size - 2)
     own_at = pl.ds(pl.multiple_of(column * half, half), half)
     other_at = pl.ds(pl.multiple_of(partner * half, half), half)
     rows = half // CHUNKS
@@ -138,9 +146,12 @@
     greet((place, partner))
     pl.when(has_left)(lambda: greet((below, column)))
     pl.when(has_right)(lambda: greet((above, column)))
-    pl.semaphore_wait(barrier, 1 + has_left.astype(jnp.int32) + has_right.astype(jnp.int32))
-
-    targets = {"above": (above, column), "below": (below, column), "partner": (place, partner)}
+    pl.when(even_left)(lambda: greet((under, column)))
+    pl.when(even_right)(lambda: greet((over, column)))
+    peers = [x.astype(jnp.int32) for x in (has_left, has_right, even_left, even_right)]
+    pl.semaphore_wait(barrier, 1 + peers[0] + peers[1] + peers[2] + peers[3])
+
+    targets = {"above": (above, column), "below": (below, column), "partner": (place, partner), "over": (over, column)}
 
     def copy(slot, source, target, chunk=None):
         sem = CHUNKS * slot + (chunk or 0)
@@ -228,9 +239,9 @@
     c_uao = copy(11, bufs.at[9], "partner")
     c_za = [copy(12, zown.at[1], "below", i) for i in range(CHUNKS)]
     c_zao = [copy(13, bufs.at[12], "partner", i) for i in range(CHUNKS)]
-    c_ul1 = copy(14, cur.at[1], "above")
-    c_fl1 = copy(15, cur.at[2], "above")
-    c_zl1 = [copy(16, zown.at[1], "above", i) for i in range(CHUNKS)]
+    c_ul1 = copy(14, bufs.at[9], "over")
+    c_fl1 = copy(15, bufs.at[10], "over")
+    c_zl1 = [copy(16, bufs.at[12], "over", i) for i in range(CHUNKS)]
     c_zl1o = [copy(17, bufs.at[16], "partner", i) for i in range(CHUNKS)]
 
     @pl.when(odd)
@@ -238,12 +249,6 @@
         c_do1.start()
         c_ua.start()
         c_fa.start()
-
-        @pl.when(has_right)
-        def _():
-            c_ul1.start()
-            c_fl1.start()
-
         c_do1.wait_recv()
         assemble(s_ref, cur.at[0], bufs.at[7])
         invert(s_ref, tile_ref)
@@ -251,11 +256,6 @@
         for i in c_za:
             i.start()
 
-        @pl.when(has_right)
-        def _():
-            for i in c_zl1:
-                i.start()
-
         dout_ref[0] = cur[0]
         uout_ref[0] = cur[1]
         fout_ref[0] = cur[2]
@@ -268,14 +268,17 @@
     def _():
         c_uo1.start()
         c_ua.wait_recv()
+        pl.when(even_right)(c_ul1.start)
         c_uao.start()
         c_uo1.wait_recv()
         assemble(full_ref, cur.at[1], bufs.at[8])
         uout_ref[0] = cur[1]
         c_fa.wait_recv()
+        pl.when(even_right)(c_fl1.start)
         c_uao.wait_recv()
         for i in range(CHUNKS):
             c_za[i].wait_recv()
+            pl.when(even_right)(c_zl1[i].start)
             c_zao[i].start()
         for i in range(CHUNKS):
             c_zao[i].wait_recv()
@@ -305,7 +308,7 @@
     drained(has_right, [c_ul, c_fl] + c_zl)
     drained(has_left, c_zlo)
     drained(odd, [c_do1, c_ua, c_fa] + c_za)
-    drained(odd_right, [c_ul1, c_fl1] + c_zl1)
+    drained(even_right, [c_ul1, c_fl1] + c_zl1)
     drained(even, [c_uo1, c_uao] + c_zao)
     drained(even_left, c_zl1o)
 

time: 135 us -> 103 us (0.76); the launches traced: 135 us -> 101 us
  Pallas kernels: 131 us -> 97.5 us
    pallas_call x1, Pallas kernels: 131 us -> 97.5 us  [body(): pl.pallas_call(functools.partial(kernel, tm_size), out_shape=[jax.ShapeDt...]
where the time goes in v2:
time: 103 us; the launch traced here: 101 us
  Pallas kernels  97.5 us (95%)
  local copies, waits for them, and re-layouts  2.91 us (3%)
    pallas_call x1, Pallas kernels, body(): pl.pallas_call(functools.partial(kernel, tm_size), out_shape=[jax.ShapeDt...  97.5 us
    unnamed x3, local copies, waits for them, and re-layouts  2.91 us

profile of v2, /device:TPU:12, one launch (start us, length us, event | category | flops | bytes accessed | tf_op | source)
XLA Modules:
  0.0 101.1 jit_solution(17312872581870483226)
XLA Ops:
  0.6 97.5 %reduce_levels.1 = (f32[2,256,512]{2,1,0:T(8,128)S(1)}, f32[2,256,512]{2,1,0:T(8,128)S(1)}, f32[2,256,512]{2,1,0:T(8,128)S(1)}) custom-call(f32[2,256,512]{2,1,0:T(8,128)} %d_ref.1, f32[2,256,512]{2,1,0:T(8,128)} %u_ref.1, f32[2,256,512]{2,1,0:T(8,128)} %f_ref.1), custom_call_target="tpu_custom_call" | custom-call | tf_op jit(solution)/shard_map/reduce_levels/pallas_call | solution.py:323
  98.2 1.0 copy.9
  99.1 1.0 copy.10
  100.1 1.0 copy.11
